TPU v7x, 32 devices: a whole 2x2x4 slice. The times are simulated.
32 devices in a mesh: runs: 2 (over y), ja: 16 (over z, x, core).
Axes of the slice: x: 2, y: 2, z: 4, core: 2. Of those that a mesh axis runs over, the one named last changes fastest.
Arguments:
- pos_vel: float32 [6, 32768], P(None, ('runs', 'ja')), parts along dimension 1, may hold values from -4 to 4
- acc_jerk: float32 [6, 32768], P(None, ('runs', 'ja')), parts along dimension 1, may hold values from -5 to 5
- star_mass: float32 [32768], P(('runs', 'ja')), parts along dimension 0, may hold values from 1.2207031e-05 to 0.00030517578
- step_phase: float32 [32768], P(('runs', 'ja')), parts along dimension 0, may hold values from 0.25 to 1
- step_level: int32 [32768], P(('runs', 'ja')), parts along dimension 0, may hold values from 0 to 3
- counts: int32 [32], P(('runs', 'ja')), parts along dimension 0, may hold values from 1 to 256, 2048 in all
- star_order: int32 [32, 1024], P(('runs', 'ja')), parts along dimension 0, may hold values from 0 to 1023, each once within a row
Outputs:
- new_pos_vel: float32 [6, 32768], P(None, ('runs', 'ja')), parts along dimension 1
- new_acc_jerk: float32 [6, 32768], P(None, ('runs', 'ja')), parts along dimension 1
- active_state: float32 [12, 8192], P(None, ('runs', 'ja')), parts along dimension 1
There are 2 independent parts, one for each index of `runs`. A program takes and returns all parts, laid end to end along the dimension named above; each array names one. Nothing has to cross between parts.
Inputs may be any that keep to these rules, and one draw needn't show every extreme that they name: The counts sum to 2048; the largest is exactly 256. `star_order`: each row is a permutation of the local indices.
All inputs are finite; a program needn't handle non-finite values. No bound on the sum of `counts` on one device may be relied on, other than what follows from the above.
Results may differ from a plain program's by a relative error of at most 0.00002.
Values sent between devices are 32-bit elements; how exact they have to be, the bound alone decides.
A program may use at most 64 MiB of HBM per device.

v0:
```python
import math
import jax
import jax.numpy as jnp
from jax import lax
from jax.sharding import PartitionSpec as P

A_DEV = 128
soft_sq = 0.01
base_step = 2.0


def predict(pos_vel, acc_jerk, age):
    half_sq = 0.5 * age * age
    sixth_cube = age * age * age / 6.0
    position = (
        pos_vel[0:3] + age * pos_vel[3:6] + half_sq * acc_jerk[0:3] + sixth_cube * acc_jerk[3:6]
    )
    velocity = pos_vel[3:6] + age * acc_jerk[0:3] + half_sq * acc_jerk[3:6]
    return jnp.concatenate([position, velocity], axis=0)


def pair_block(targets, sources):
    delta_x = sources[0:3, None, :] - targets[0:3, :, None]
    delta_v = sources[3:6, None, :] - targets[3:6, :, None]
    dist_sq = soft_sq + delta_x[0] * delta_x[0] + delta_x[1] * delta_x[1] + delta_x[2] * delta_x[2]
    inverse = lax.rsqrt(dist_sq)
    inverse_sq = inverse * inverse
    weight = sources[6][None, :] * inverse * inverse_sq
    radial = (
        3.0
        * (delta_x[0] * delta_v[0] + delta_x[1] * delta_v[1] + delta_x[2] * delta_v[2])
        * inverse_sq
    )
    accel_part = jnp.sum(weight[None] * delta_x, axis=2)
    jerk_part = jnp.sum(weight[None] * (delta_v - radial[None] * delta_x), axis=2)
    return jnp.concatenate([accel_part, jerk_part], axis=0)


def pair_forces(targets, sources):
    rows = targets.shape[1]
    block = math.gcd(rows, 512)
    split = targets.reshape(6, rows // block, block).transpose(1, 0, 2)
    result = lax.map(lambda part: pair_block(part, sources), split)
    return result.transpose(1, 0, 2).reshape(6, rows)


def correct(old_pv, old_aj, fresh, step_len):
    half = 0.5 * step_len
    twelfth = step_len * step_len / 12.0
    velocity = (
        old_pv[3:6] + half * (old_aj[0:3] + fresh[0:3]) + twelfth * (old_aj[3:6] - fresh[3:6])
    )
    position = old_pv[0:3] + half * (old_pv[3:6] + velocity) + twelfth * (old_aj[0:3] - fresh[0:3])
    return jnp.concatenate([position, velocity], axis=0)


def per_device(pos_vel, acc_jerk, star_mass, step_phase, step_level, counts, star_order):
    capacity = 2 * A_DEV
    per_owner = pos_vel.shape[1]
    slot_ids = star_order[0, :capacity]
    live = jnp.arange(capacity, dtype=jnp.int32) < counts[0]
    step_len = base_step * jnp.exp2(-step_level.astype(jnp.float32))
    is_active = jnp.zeros((per_owner,), jnp.float32).at[slot_ids].set(live.astype(jnp.float32))
    age = step_len * jnp.where(is_active > 0.5, jnp.float32(1.0), step_phase)
    predicted = predict(pos_vel, acc_jerk, age)
    sources = jnp.concatenate([predicted, star_mass[None, :]], axis=0)
    targets = predicted[:, slot_ids]
    every_slot = pair_forces(lax.all_gather(targets, "ja", axis=1, tiled=True), sources)
    fresh = lax.psum_scatter(every_slot, "ja", scatter_dimension=1, tiled=True)
    old_pv = pos_vel[:, slot_ids]
    old_aj = acc_jerk[:, slot_ids]
    corrected = correct(old_pv, old_aj, fresh, step_len[slot_ids])
    kept_pv = jnp.where(live[None, :], corrected, old_pv)
    kept_aj = jnp.where(live[None, :], fresh, old_aj)
    fresh_state = jnp.concatenate([corrected, fresh], axis=0)
    active_state = jnp.where(live[None, :], fresh_state, jnp.zeros_like(fresh_state))
    return (
        pos_vel.at[:, slot_ids].set(kept_pv),
        acc_jerk.at[:, slot_ids].set(kept_aj),
        active_state,
    )


def solution(mesh):
    in_specs = (
        P(None, ("runs", "ja")),
        P(None, ("runs", "ja")),
        P(("runs", "ja")),
        P(("runs", "ja")),
        P(("runs", "ja")),
        P(("runs", "ja")),
        P(("runs", "ja"), None),
    )
    out_specs = (P(None, ("runs", "ja")), P(None, ("runs", "ja")), P(None, ("runs", "ja")))
    return jax.shard_map(
        per_device, mesh=mesh, in_specs=in_specs, out_specs=out_specs, check_vma=False
    )
```

profile of v0, /device:TPU:0, one launch (start us, length us, event | category | flops | bytes accessed | tf_op | source)
XLA Modules:
  0.0 163.4 jit_solution(9039283092665602739)
XLA Ops:
  7.2 0.7 compare_select_fusion
  8.6 1.4 scatter_custom_fusion
  10.0 0.7 multiply_multiply_fusion.1
  10.7 0.9 multiply_add_fusion
  11.6 0.2 copy.81
  11.8 0.7 gather_fusion.3
  12.6 32.3 %all-gather = f32[6,4096]{0,1:T(8,128)S(1)} all-gather(f32[6,256]{0,1:T(8,128)S(1)} %bitcast.44), channel_id=2, replica_groups=mesh['runs'=2,'ja'=16] {'ja'}, dimensions={1}, use_global_device_ids=true | all-gather | bytes 104448 | tf_op jit(solution)/shard_map/all_gather | solution.py:68
  44.8 0.6 copy.82
  45.5 45.8 %while.10 = (s32[]{:T(128)}, f32[8,6,512]{2,1,0:T(8,128)S(1)}, f32[1,1024]{1,0:T(1,128)S(1)}, f32[3,1024]{1,0:T(4,128)S(1)}, f32[8,6,512]{2,1,0:T(8,128)S(1)}, /...) while((s32[]{:T(128)}, f32[8,6,512]{2,1,0:T(8,128)S(1)}, f32[1,1024]{1,0:T(1,128)S(1)}, ...), condition=%wide.region_4.5_spmd, body=%wide.region_1.4_spmd.sunk | while | flops 24117252 | bytes 33702004 | solution.py:43
  45.5 1.1 broadcast_subtract_fusion.3
  46.6 2.1 %fusion.17 = (f32[512,1024]{1,0:T(8,128)S(1)}, f32[512,1024]{1,0:T(8,128)S(1)}) fusion(f32[3,512,1024]{2,1,0:T(8,128)S(1)} %get-tuple-element.141, f32[3,512,1024]{2,1,0:T(8,128)S(1)} %get-tuple-element.142, f32[1024]{0:T(1024)S(1)} %bitcast.47), kind=kLoop, calls=%fused_computation.15.clone.1 | loop fusion | flops 8388608 | bytes 16781312 | tf_op jit(solution)/shard_map/while/body/eval_jaxpr/mul | solution.py:35
  48.7 2.5 %multiply_reduce_fusion.3 = (f32[3,512]{1,0:T(4,128)S(1)}, f32[3,512]{1,0:T(4,128)S(1)}) fusion(f32[512,1024]{1,0:T(8,128)S(1)} %get-tuple-element.143, f32[3,512]{1,0:T(4,128)S(1)} %get-tuple-element.140, f32[3,1024]{1,0:T(4,128)S(1)} %get-tuple-element.168, f32[512,1024]{1,0:T(8,128)S(1)} %get-tuple-element.144, ...), kind=kLoop, calls=%fused_computation.8.clone.1 | loop fusion | flops 12579840 | bytes 4243456 | tf_op jit(solution)/shard_map/while/body/eval_jaxpr/reduce_sum | solution.py:34
  51.2 1.1 broadcast_subtract_fusion.3
  52.3 2.1 %fusion.17 = (f32[512,1024]{1,0:T(8,128)S(1)}, f32[512,1024]{1,0:T(8,128)S(1)}) fusion(f32[3,512,1024]{2,1,0:T(8,128)S(1)} %get-tuple-element.141, f32[3,512,1024]{2,1,0:T(8,128)S(1)} %get-tuple-element.142, f32[1024]{0:T(1024)S(1)} %bitcast.47), kind=kLoop, calls=%fused_computation.15.clone.1 | loop fusion | flops 8388608 | bytes 16781312 | tf_op jit(solution)/shard_map/while/body/eval_jaxpr/mul | solution.py:35
  54.4 2.5 %multiply_reduce_fusion.3 = (f32[3,512]{1,0:T(4,128)S(1)}, f32[3,512]{1,0:T(4,128)S(1)}) fusion(f32[512,1024]{1,0:T(8,128)S(1)} %get-tuple-element.143, f32[3,512]{1,0:T(4,128)S(1)} %get-tuple-element.140, f32[3,1024]{1,0:T(4,128)S(1)} %get-tuple-element.168, f32[512,1024]{1,0:T(8,128)S(1)} %get-tuple-element.144, ...), kind=kLoop, calls=%fused_computation.8.clone.1 | loop fusion | flops 12579840 | bytes 4243456 | tf_op jit(solution)/shard_map/while/body/eval_jaxpr/reduce_sum | solution.py:34
  57.0 1.1 broadcast_subtract_fusion.3
  58.0 2.1 %fusion.17 = (f32[512,1024]{1,0:T(8,128)S(1)}, f32[512,1024]{1,0:T(8,128)S(1)}) fusion(f32[3,512,1024]{2,1,0:T(8,128)S(1)} %get-tuple-element.141, f32[3,512,1024]{2,1,0:T(8,128)S(1)} %get-tuple-element.142, f32[1024]{0:T(1024)S(1)} %bitcast.47), kind=kLoop, calls=%fused_computation.15.clone.1 | loop fusion | flops 8388608 | bytes 16781312 | tf_op jit(solution)/shard_map/while/body/eval_jaxpr/mul | solution.py:35
  60.1 2.5 %multiply_reduce_fusion.3 = (f32[3,512]{1,0:T(4,128)S(1)}, f32[3,512]{1,0:T(4,128)S(1)}) fusion(f32[512,1024]{1,0:T(8,128)S(1)} %get-tuple-element.143, f32[3,512]{1,0:T(4,128)S(1)} %get-tuple-element.140, f32[3,1024]{1,0:T(4,128)S(1)} %get-tuple-element.168, f32[512,1024]{1,0:T(8,128)S(1)} %get-tuple-element.144, ...), kind=kLoop, calls=%fused_computation.8.clone.1 | loop fusion | flops 12579840 | bytes 4243456 | tf_op jit(solution)/shard_map/while/body/eval_jaxpr/reduce_sum | solution.py:34
  62.7 1.1 broadcast_subtract_fusion.3
  63.8 2.1 %fusion.17 = (f32[512,1024]{1,0:T(8,128)S(1)}, f32[512,1024]{1,0:T(8,128)S(1)}) fusion(f32[3,512,1024]{2,1,0:T(8,128)S(1)} %get-tuple-element.141, f32[3,512,1024]{2,1,0:T(8,128)S(1)} %get-tuple-element.142, f32[1024]{0:T(1024)S(1)} %bitcast.47), kind=kLoop, calls=%fused_computation.15.clone.1 | loop fusion | flops 8388608 | bytes 16781312 | tf_op jit(solution)/shard_map/while/body/eval_jaxpr/mul | solution.py:35
  65.8 2.5 %multiply_reduce_fusion.3 = (f32[3,512]{1,0:T(4,128)S(1)}, f32[3,512]{1,0:T(4,128)S(1)}) fusion(f32[512,1024]{1,0:T(8,128)S(1)} %get-tuple-element.143, f32[3,512]{1,0:T(4,128)S(1)} %get-tuple-element.140, f32[3,1024]{1,0:T(4,128)S(1)} %get-tuple-element.168, f32[512,1024]{1,0:T(8,128)S(1)} %get-tuple-element.144, ...), kind=kLoop, calls=%fused_computation.8.clone.1 | loop fusion | flops 12579840 | bytes 4243456 | tf_op jit(solution)/shard_map/while/body/eval_jaxpr/reduce_sum | solution.py:34
  68.4 1.1 broadcast_subtract_fusion.3
  69.5 2.1 %fusion.17 = (f32[512,1024]{1,0:T(8,128)S(1)}, f32[512,1024]{1,0:T(8,128)S(1)}) fusion(f32[3,512,1024]{2,1,0:T(8,128)S(1)} %get-tuple-element.141, f32[3,512,1024]{2,1,0:T(8,128)S(1)} %get-tuple-element.142, f32[1024]{0:T(1024)S(1)} %bitcast.47), kind=kLoop, calls=%fused_computation.15.clone.1 | loop fusion | flops 8388608 | bytes 16781312 | tf_op jit(solution)/shard_map/while/body/eval_jaxpr/mul | solution.py:35
  71.6 2.5 %multiply_reduce_fusion.3 = (f32[3,512]{1,0:T(4,128)S(1)}, f32[3,512]{1,0:T(4,128)S(1)}) fusion(f32[512,1024]{1,0:T(8,128)S(1)} %get-tuple-element.143, f32[3,512]{1,0:T(4,128)S(1)} %get-tuple-element.140, f32[3,1024]{1,0:T(4,128)S(1)} %get-tuple-element.168, f32[512,1024]{1,0:T(8,128)S(1)} %get-tuple-element.144, ...), kind=kLoop, calls=%fused_computation.8.clone.1 | loop fusion | flops 12579840 | bytes 4243456 | tf_op jit(solution)/shard_map/while/body/eval_jaxpr/reduce_sum | solution.py:34
  74.1 1.1 broadcast_subtract_fusion.3
  75.2 2.1 %fusion.17 = (f32[512,1024]{1,0:T(8,128)S(1)}, f32[512,1024]{1,0:T(8,128)S(1)}) fusion(f32[3,512,1024]{2,1,0:T(8,128)S(1)} %get-tuple-element.141, f32[3,512,1024]{2,1,0:T(8,128)S(1)} %get-tuple-element.142, f32[1024]{0:T(1024)S(1)} %bitcast.47), kind=kLoop, calls=%fused_computation.15.clone.1 | loop fusion | flops 8388608 | bytes 16781312 | tf_op jit(solution)/shard_map/while/body/eval_jaxpr/mul | solution.py:35
  77.3 2.5 %multiply_reduce_fusion.3 = (f32[3,512]{1,0:T(4,128)S(1)}, f32[3,512]{1,0:T(4,128)S(1)}) fusion(f32[512,1024]{1,0:T(8,128)S(1)} %get-tuple-element.143, f32[3,512]{1,0:T(4,128)S(1)} %get-tuple-element.140, f32[3,1024]{1,0:T(4,128)S(1)} %get-tuple-element.168, f32[512,1024]{1,0:T(8,128)S(1)} %get-tuple-element.144, ...), kind=kLoop, calls=%fused_computation.8.clone.1 | loop fusion | flops 12579840 | bytes 4243456 | tf_op jit(solution)/shard_map/while/body/eval_jaxpr/reduce_sum | solution.py:34
  79.8 1.1 broadcast_subtract_fusion.3
  80.9 2.1 %fusion.17 = (f32[512,1024]{1,0:T(8,128)S(1)}, f32[512,1024]{1,0:T(8,128)S(1)}) fusion(f32[3,512,1024]{2,1,0:T(8,128)S(1)} %get-tuple-element.141, f32[3,512,1024]{2,1,0:T(8,128)S(1)} %get-tuple-element.142, f32[1024]{0:T(1024)S(1)} %bitcast.47), kind=kLoop, calls=%fused_computation.15.clone.1 | loop fusion | flops 8388608 | bytes 16781312 | tf_op jit(solution)/shard_map/while/body/eval_jaxpr/mul | solution.py:35
  83.0 2.5 %multiply_reduce_fusion.3 = (f32[3,512]{1,0:T(4,128)S(1)}, f32[3,512]{1,0:T(4,128)S(1)}) fusion(f32[512,1024]{1,0:T(8,128)S(1)} %get-tuple-element.143, f32[3,512]{1,0:T(4,128)S(1)} %get-tuple-element.140, f32[3,1024]{1,0:T(4,128)S(1)} %get-tuple-element.168, f32[512,1024]{1,0:T(8,128)S(1)} %get-tuple-element.144, ...), kind=kLoop, calls=%fused_computation.8.clone.1 | loop fusion | flops 12579840 | bytes 4243456 | tf_op jit(solution)/shard_map/while/body/eval_jaxpr/reduce_sum | solution.py:34
  85.6 1.1 broadcast_subtract_fusion.3
  86.6 2.1 %fusion.17 = (f32[512,1024]{1,0:T(8,128)S(1)}, f32[512,1024]{1,0:T(8,128)S(1)}) fusion(f32[3,512,1024]{2,1,0:T(8,128)S(1)} %get-tuple-element.141, f32[3,512,1024]{2,1,0:T(8,128)S(1)} %get-tuple-element.142, f32[1024]{0:T(1024)S(1)} %bitcast.47), kind=kLoop, calls=%fused_computation.15.clone.1 | loop fusion | flops 8388608 | bytes 16781312 | tf_op jit(solution)/shard_map/while/body/eval_jaxpr/mul | solution.py:35
  88.7 2.5 %multiply_reduce_fusion.3 = (f32[3,512]{1,0:T(4,128)S(1)}, f32[3,512]{1,0:T(4,128)S(1)}) fusion(f32[512,1024]{1,0:T(8,128)S(1)} %get-tuple-element.143, f32[3,512]{1,0:T(4,128)S(1)} %get-tuple-element.140, f32[3,1024]{1,0:T(4,128)S(1)} %get-tuple-element.168, f32[512,1024]{1,0:T(8,128)S(1)} %get-tuple-element.144, ...), kind=kLoop, calls=%fused_computation.8.clone.1 | loop fusion | flops 12579840 | bytes 4243456 | tf_op jit(solution)/shard_map/while/body/eval_jaxpr/reduce_sum | solution.py:34
  91.3 0.6 copy-done.2
  91.9 1.4 gather_fusion.1
  93.3 0.2 copy.79
  93.6 0.2 copy.83
  93.8 0.7 gather_fusion.2
  94.6 0.7 gather_fusion
  95.4 53.7 %reduce-scatter.2.cloned.1.call-done = f32[6,256]{1,0:T(8,128)} async-done(((f32[6,4096]{1,0:T(8,128)}), f32[6,256]{1,0:T(8,128)}) %reduce-scatter.2.cloned.1.call-update) | async-done | bytes 6160 | tf_op jit(solution)/shard_map/reduce_scatter | solution.py:69
  149.1 0.8 fusion.10
  149.9 0.7 select_bitcast_fusion
  150.6 0.1 copy.86
  150.7 1.4 scatter_fusion.1
  152.1 0.8 copy.88
  153.0 1.4 scatter_fusion
  154.4 0.8 copy.87
  155.2 1.3 maximum_select_fusion
  (35 shorter events, 0.6 us)
Async XLA Ops:
  7.2 141.9 %reduce-scatter.2.cloned.1.call-start = ((), (), s32[]{:S(2)}) async-start(), calls=%async_computation.1 | async-start | bytes 139264 | tf_op jit(solution)/shard_map/reduce_scatter | solution.py:69
  12.6 32.9 %copy-start.3 = (f32[1024]{0:T(1024)S(1)}, f32[1024]{0:T(1024)}, u32[]{:S(2)}) copy-start(f32[1024]{0:T(1024)} %param.11) | copy-start | bytes 12292
  45.5 47.8 %copy-start = (f32[6,1024]{1,0:T(8,128)S(1)}, f32[6,1024]{1,0:T(8,128)}, u32[]{:S(2)}) copy-start(f32[6,1024]{1,0:T(8,128)} %param.10) | copy-start | bytes 73732
  45.5 48.1 %copy-start.1 = (f32[6,1024]{1,0:T(8,128)S(1)}, f32[6,1024]{1,0:T(8,128)}, u32[]{:S(2)}) copy-start(f32[6,1024]{1,0:T(8,128)} %param.9) | copy-start | bytes 73732
  91.2 0.6 copy-start.2
Sparse Core Ops, SparseCore 0:
  92.0 56.9 reduce-scatter.1
where the time goes:
time: 164 us; the launch traced here: 163 us
  waiting for transfers between devices  53.7 us (33%)
  other arithmetic  50.4 us (31%)
  blocking collectives  32.3 us (20%)
  between operations  14.8 us (9%)
  local copies, waits for them, and re-layouts  11.8 us (7%)
    reduce_scatter x1, waiting for transfers between devices, per_device(): fresh = lax.psum_scatter(every_slot, 'ja', scatter_dimension=1, tiled=True)  53.7 us
    all_gather x1, blocking collectives, per_device(): lax.all_gather(targets, 'ja', axis=1, tiled=True)  32.3 us
    reduce_sum x8, other arithmetic, pair_block(): accel_part = jnp.sum(weight[None] * delta_x, axis=2)  20 us
    mul x8, other arithmetic, pair_block(): radial[None] * delta_x  16.6 us
    sub x8, other arithmetic, pair_block(): delta_v = sources[3:6, None, :] - targets[3:6, :, None]  8.53 us
  transfers between devices with their start and end apart: 1, of which 1 were waited for; matrix products, arithmetic and copies ran while one was open for 2% of the time, Pallas kernels for 0%

commit v1 on v0

--- a/solution.py
+++ b/solution.py
@@ -7,6 +7,28 @@
 A_DEV = 128
 soft_sq = 0.01
 base_step = 2.0
+
+
+def joined_along(parts, dim):
+    shape = list(parts.shape[1:])
+    shape[dim] *= parts.shape[0]
+    return jnp.moveaxis(parts, 0, dim).reshape(shape)
+
+
+def gather_around(x, axis, dim):
+    peers = lax.axis_size(axis)
+    pairs = [(i, (i + 1) % peers) for i in range(peers)]
+    back = [(b, a) for a, b in pairs]
+    lower, upper = ([], [])
+    for step in range(peers - 1):
+        if step % 2 == 0:
+            lower.append(lax.ppermute(lower[-1] if lower else x, axis, pairs))
+        else:
+            upper.append(lax.ppermute(upper[-1] if upper else x, axis, back))
+    blocks = jnp.stack([*lower[::-1], x, *upper])
+    shift = lax.axis_index(axis) - len(lower)
+    blocks = blocks[(jnp.arange(peers) - shift) % peers]
+    return joined_along(blocks, dim)
 
 
 def predict(pos_vel, acc_jerk, age):
@@ -65,7 +87,7 @@
     predicted = predict(pos_vel, acc_jerk, age)
     sources = jnp.concatenate([predicted, star_mass[None, :]], axis=0)
     targets = predicted[:, slot_ids]
-    every_slot = pair_forces(lax.all_gather(targets, "ja", axis=1, tiled=True), sources)
+    every_slot = pair_forces(gather_around(targets, "ja", 1), sources)
     fresh = lax.psum_scatter(every_slot, "ja", scatter_dimension=1, tiled=True)
     old_pv = pos_vel[:, slot_ids]
     old_aj = acc_jerk[:, slot_ids]

time: 164 us -> 192 us (1.17)
  blocking collectives: 32.3 us -> 0 us
  starting transfers between devices: 0.04 us -> 31.9 us
  waiting for transfers between devices: 53.7 us -> 78.1 us
  local copies, waits for them, and re-layouts: 11.8 us -> 16.2 us
    all_gather x1 -> x0, blocking collectives: 32.3 us -> none  [per_device(): lax.all_gather(targets, 'ja', axis=1, tiled=True)]
    ppermute x0 -> x15, starting transfers between devices: none -> 31.8 us  [the longest x7 31.3 us: gather_around(): upper.append(lax.ppermute(upper[-1] if upper else x, axis, back))]
    ppermute x0 -> x15, waiting for transfers between devices: none -> 25.1 us  [the longest x8 25.1 us: gather_around(): lower.append(lax.ppermute(lower[-1] if lower else x, axis, pairs))]
    unnamed x12 -> x37, local copies, waits for them, and re-layouts: 2.7 us -> 6.55 us
  transfers between devices with their start and end apart: 1 -> 16, of which waited for: 1 -> 9; matrix products, arithmetic and copies ran while one was open for 2% -> 4% of each run, Pallas kernels for 0% -> 0%
where the time goes in v1:
time: 192 us; the launch traced here: 191 us
  waiting for transfers between devices  78.1 us (41%)
  other arithmetic  49.9 us (26%)
  starting transfers between devices  31.9 us (17%)
  local copies, waits for them, and re-layouts  16.2 us (8%)
  between operations  15.1 us (8%)
    reduce_scatter x1, waiting for transfers between devices, per_device(): fresh = lax.psum_scatter(every_slot, 'ja', scatter_dimension=1, tiled=True)  52.9 us
    ppermute x7, starting transfers between devices, gather_around(): upper.append(lax.ppermute(upper[-1] if upper else x, axis, back))  31.3 us
    ppermute x8, waiting for transfers between devices, gather_around(): lower.append(lax.ppermute(lower[-1] if lower else x, axis, pairs))  25.1 us
    reduce_sum x8, other arithmetic, pair_block(): accel_part = jnp.sum(weight[None] * delta_x, axis=2)  19.5 us
    mul x8, other arithmetic, pair_block(): radial[None] * delta_x  16.6 us
    sub x8, other arithmetic, pair_block(): delta_v = sources[3:6, None, :] - targets[3:6, :, None]  8.53 us
    unnamed x37, local copies, waits for them, and re-layouts  6.55 us
  transfers between devices with their start and end apart: 16, of which 9 were waited for; matrix products, arithmetic and copies ran while one was open for 4% of the time, Pallas kernels for 0%

profile of v1, /device:TPU:0, one launch (start us, length us, event | category | flops | bytes accessed | tf_op | source)
XLA Modules:
  0.0 191.5 jit_solution(10558629846780840214)
XLA Ops:
  8.6 1.4 scatter_custom_fusion
  13.1 7.6 %collective-permute-done = f32[6,256]{0,1:T(8,128)S(1)} collective-permute-done((f32[6,256]{0,1:T(8,128)S(1)}, f32[6,256]{0,1:T(8,128)S(1)}, u32[]{:S(2)}, u32[]{:S(2)}) %collective-permute-start) | collective-permute-done | bytes 6176 | tf_op jit(solution)/shard_map/ppermute | solution.py:25
  20.7 4.4 %collective-permute-start.8 = (f32[6,256]{0,1:T(8,128)S(1)}, f32[6,256]{0,1:T(8,128)S(1)}, u32[]{:S(2)}, u32[]{:S(2)}) collective-permute-start(f32[6,256]{0,1:T(8,128)S(1)} %bitcast.82), channel_id=1, source_target_pairs={{1,0},{2,1},{3,2},{4,3},{5,4},{6,5},{7,6},{8,7},{9,8},{10,9},{11,1... | collective-permute-start | bytes 18440 | tf_op jit(solution)/shard_map/ppermute | solution.py:27
  25.1 2.7 %collective-permute-done.1 = f32[6,256]{0,1:T(8,128)S(1)} collective-permute-done((f32[6,256]{0,1:T(8,128)S(1)}, f32[6,256]{0,1:T(8,128)S(1)}, u32[]{:S(2)}, u32[]{:S(2)}) %collective-permute-start.1) | collective-permute-done | bytes 6176 | tf_op jit(solution)/shard_map/ppermute | solution.py:25
  27.8 4.5 %collective-permute-start.9 = (f32[6,256]{0,1:T(8,128)S(1)}, f32[6,256]{0,1:T(8,128)S(1)}, u32[]{:S(2)}, u32[]{:S(2)}) collective-permute-start(f32[6,256]{0,1:T(8,128)S(1)} %collective-permute-done.8), channel_id=1, source_target_pairs={{1,0},{2,1},{3,2},{4,3},{5,4},{6,5},{7,6},{8,7},{9,8},{10,9},{11,1... | collective-permute-start | bytes 18440 | tf_op jit(solution)/shard_map/ppermute | solution.py:27
  32.3 2.7 %collective-permute-done.2 = f32[6,256]{0,1:T(8,128)S(1)} collective-permute-done((f32[6,256]{0,1:T(8,128)S(1)}, f32[6,256]{0,1:T(8,128)S(1)}, u32[]{:S(2)}, u32[]{:S(2)}) %collective-permute-start.2) | collective-permute-done | bytes 6176 | tf_op jit(solution)/shard_map/ppermute | solution.py:25
  35.0 4.4 %collective-permute-start.10 = (f32[6,256]{0,1:T(8,128)S(1)}, f32[6,256]{0,1:T(8,128)S(1)}, u32[]{:S(2)}, u32[]{:S(2)}) collective-permute-start(f32[6,256]{0,1:T(8,128)S(1)} %collective-permute-done.9), channel_id=1, source_target_pairs={{1,0},{2,1},{3,2},{4,3},{5,4},{6,5},{7,6},{8,7},{9,8},{10,9},{11,1... | collective-permute-start | bytes 18440 | tf_op jit(solution)/shard_map/ppermute | solution.py:27
  39.4 2.7 %collective-permute-done.3 = f32[6,256]{0,1:T(8,128)S(1)} collective-permute-done((f32[6,256]{0,1:T(8,128)S(1)}, f32[6,256]{0,1:T(8,128)S(1)}, u32[]{:S(2)}, u32[]{:S(2)}) %collective-permute-start.3) | collective-permute-done | bytes 6176 | tf_op jit(solution)/shard_map/ppermute | solution.py:25
  42.2 4.4 %collective-permute-start.11 = (f32[6,256]{0,1:T(8,128)S(1)}, f32[6,256]{0,1:T(8,128)S(1)}, u32[]{:S(2)}, u32[]{:S(2)}) collective-permute-start(f32[6,256]{0,1:T(8,128)S(1)} %collective-permute-done.10), channel_id=1, source_target_pairs={{1,0},{2,1},{3,2},{4,3},{5,4},{6,5},{7,6},{8,7},{9,8},{10,9},{11,1... | collective-permute-start | bytes 18440 | tf_op jit(solution)/shard_map/ppermute | solution.py:27
  46.6 2.7 %collective-permute-done.4 = f32[6,256]{0,1:T(8,128)S(1)} collective-permute-done((f32[6,256]{0,1:T(8,128)S(1)}, f32[6,256]{0,1:T(8,128)S(1)}, u32[]{:S(2)}, u32[]{:S(2)}) %collective-permute-start.4) | collective-permute-done | bytes 6176 | tf_op jit(solution)/shard_map/ppermute | solution.py:25
  49.4 4.4 %collective-permute-start.12 = (f32[6,256]{0,1:T(8,128)S(1)}, f32[6,256]{0,1:T(8,128)S(1)}, u32[]{:S(2)}, u32[]{:S(2)}) collective-permute-start(f32[6,256]{0,1:T(8,128)S(1)} %collective-permute-done.11), channel_id=1, source_target_pairs={{1,0},{2,1},{3,2},{4,3},{5,4},{6,5},{7,6},{8,7},{9,8},{10,9},{11,1... | collective-permute-start | bytes 18440 | tf_op jit(solution)/shard_map/ppermute | solution.py:27
  53.8 2.7 %collective-permute-done.5 = f32[6,256]{0,1:T(8,128)S(1)} collective-permute-done((f32[6,256]{0,1:T(8,128)S(1)}, f32[6,256]{0,1:T(8,128)S(1)}, u32[]{:S(2)}, u32[]{:S(2)}) %collective-permute-start.5) | collective-permute-done | bytes 6176 | tf_op jit(solution)/shard_map/ppermute | solution.py:25
  56.6 4.5 %collective-permute-start.13 = (f32[6,256]{0,1:T(8,128)S(1)}, f32[6,256]{0,1:T(8,128)}, u32[]{:S(2)}, u32[]{:S(2)}) collective-permute-start(f32[6,256]{0,1:T(8,128)S(1)} %collective-permute-done.12), channel_id=1, source_target_pairs={{1,0},{2,1},{3,2},{4,3},{5,4},{6,5},{7,6},{8,7},{9,8},{10,9},{11,1... | collective-permute-start | bytes 18440 | tf_op jit(solution)/shard_map/ppermute | solution.py:27
  61.1 2.7 %collective-permute-done.6 = f32[6,256]{0,1:T(8,128)S(1)} collective-permute-done((f32[6,256]{0,1:T(8,128)S(1)}, f32[6,256]{0,1:T(8,128)S(1)}, u32[]{:S(2)}, u32[]{:S(2)}) %collective-permute-start.6) | collective-permute-done | bytes 6176 | tf_op jit(solution)/shard_map/ppermute | solution.py:25
  63.8 1.4 gather_fusion.1
  65.2 4.5 %collective-permute-start.14 = (f32[6,256]{0,1:T(8,128)}, f32[6,256]{0,1:T(8,128)S(1)}, u32[]{:S(2)}, u32[]{:S(2)}) collective-permute-start(f32[6,256]{0,1:T(8,128)} %collective-permute-done.13), channel_id=1, source_target_pairs={{1,0},{2,1},{3,2},{4,3},{5,4},{6,5},{7,6},{8,7},{9,8},{10,9},{11,1... | collective-permute-start | bytes 18440 | tf_op jit(solution)/shard_map/ppermute | solution.py:27
  69.7 1.3 collective-permute-done.7
  71.0 0.9 bitcast_dynamic-update-slice_fusion.15
  71.9 0.9 bitcast_dynamic-update-slice_fusion.14
  76.2 45.2 %while.10 = (s32[]{:T(128)}, f32[8,6,512]{2,1,0:T(8,128)S(1)}, f32[1,1024]{1,0:T(1,128)S(1)}, f32[3,1024]{1,0:T(4,128)S(1)}, f32[8,6,512]{2,1,0:T(8,128)S(1)}, /...) while((s32[]{:T(128)}, f32[8,6,512]{2,1,0:T(8,128)S(1)}, f32[1,1024]{1,0:T(1,128)S(1)}, ...), condition=%wide.region_4.5_spmd, body=%wide.region_1.4_spmd.sunk | while | flops 24117252 | bytes 33702004 | solution.py:65
  76.2 1.1 broadcast_subtract_fusion.3
  77.3 2.1 %fusion.19 = (f32[512,1024]{1,0:T(8,128)S(1)}, f32[512,1024]{1,0:T(8,128)S(1)}) fusion(f32[3,512,1024]{2,1,0:T(8,128)S(1)} %get-tuple-element.144, f32[3,512,1024]{2,1,0:T(8,128)S(1)} %get-tuple-element.145, f32[1024]{0:T(1024)S(1)} %bitcast.85), kind=kLoop, calls=%fused_computation.16.clone.1 | loop fusion | flops 8388608 | bytes 16781312 | tf_op jit(solution)/shard_map/while/body/eval_jaxpr/mul | solution.py:57
  79.4 2.4 %multiply_reduce_fusion.3 = (f32[3,512]{1,0:T(4,128)S(1)}, f32[3,512]{1,0:T(4,128)S(1)}) fusion(f32[512,1024]{1,0:T(8,128)S(1)} %get-tuple-element.146, f32[3,512]{1,0:T(4,128)S(1)} %get-tuple-element.143, f32[3,1024]{1,0:T(4,128)S(1)} %get-tuple-element.171, f32[512,1024]{1,0:T(8,128)S(1)} %get-tuple-element.147, ...), kind=kLoop, calls=%fused_computation.9.clone.1 | loop fusion | flops 12579840 | bytes 4243456 | tf_op jit(solution)/shard_map/while/body/eval_jaxpr/reduce_sum | solution.py:56
  81.9 1.1 broadcast_subtract_fusion.3
  83.0 2.1 %fusion.19 = (f32[512,1024]{1,0:T(8,128)S(1)}, f32[512,1024]{1,0:T(8,128)S(1)}) fusion(f32[3,512,1024]{2,1,0:T(8,128)S(1)} %get-tuple-element.144, f32[3,512,1024]{2,1,0:T(8,128)S(1)} %get-tuple-element.145, f32[1024]{0:T(1024)S(1)} %bitcast.85), kind=kLoop, calls=%fused_computation.16.clone.1 | loop fusion | flops 8388608 | bytes 16781312 | tf_op jit(solution)/shard_map/while/body/eval_jaxpr/mul | solution.py:57
  85.0 2.4 %multiply_reduce_fusion.3 = (f32[3,512]{1,0:T(4,128)S(1)}, f32[3,512]{1,0:T(4,128)S(1)}) fusion(f32[512,1024]{1,0:T(8,128)S(1)} %get-tuple-element.146, f32[3,512]{1,0:T(4,128)S(1)} %get-tuple-element.143, f32[3,1024]{1,0:T(4,128)S(1)} %get-tuple-element.171, f32[512,1024]{1,0:T(8,128)S(1)} %get-tuple-element.147, ...), kind=kLoop, calls=%fused_computation.9.clone.1 | loop fusion | flops 12579840 | bytes 4243456 | tf_op jit(solution)/shard_map/while/body/eval_jaxpr/reduce_sum | solution.py:56
  87.5 1.1 broadcast_subtract_fusion.3
  88.6 2.1 %fusion.19 = (f32[512,1024]{1,0:T(8,128)S(1)}, f32[512,1024]{1,0:T(8,128)S(1)}) fusion(f32[3,512,1024]{2,1,0:T(8,128)S(1)} %get-tuple-element.144, f32[3,512,1024]{2,1,0:T(8,128)S(1)} %get-tuple-element.145, f32[1024]{0:T(1024)S(1)} %bitcast.85), kind=kLoop, calls=%fused_computation.16.clone.1 | loop fusion | flops 8388608 | bytes 16781312 | tf_op jit(solution)/shard_map/while/body/eval_jaxpr/mul | solution.py:57
  90.7 2.4 %multiply_reduce_fusion.3 = (f32[3,512]{1,0:T(4,128)S(1)}, f32[3,512]{1,0:T(4,128)S(1)}) fusion(f32[512,1024]{1,0:T(8,128)S(1)} %get-tuple-element.146, f32[3,512]{1,0:T(4,128)S(1)} %get-tuple-element.143, f32[3,1024]{1,0:T(4,128)S(1)} %get-tuple-element.171, f32[512,1024]{1,0:T(8,128)S(1)} %get-tuple-element.147, ...), kind=kLoop, calls=%fused_computation.9.clone.1 | loop fusion | flops 12579840 | bytes 4243456 | tf_op jit(solution)/shard_map/while/body/eval_jaxpr/reduce_sum | solution.py:56
  93.2 1.1 broadcast_subtract_fusion.3
  94.3 2.1 %fusion.19 = (f32[512,1024]{1,0:T(8,128)S(1)}, f32[512,1024]{1,0:T(8,128)S(1)}) fusion(f32[3,512,1024]{2,1,0:T(8,128)S(1)} %get-tuple-element.144, f32[3,512,1024]{2,1,0:T(8,128)S(1)} %get-tuple-element.145, f32[1024]{0:T(1024)S(1)} %bitcast.85), kind=kLoop, calls=%fused_computation.16.clone.1 | loop fusion | flops 8388608 | bytes 16781312 | tf_op jit(solution)/shard_map/while/body/eval_jaxpr/mul | solution.py:57
  96.3 2.4 %multiply_reduce_fusion.3 = (f32[3,512]{1,0:T(4,128)S(1)}, f32[3,512]{1,0:T(4,128)S(1)}) fusion(f32[512,1024]{1,0:T(8,128)S(1)} %get-tuple-element.146, f32[3,512]{1,0:T(4,128)S(1)} %get-tuple-element.143, f32[3,1024]{1,0:T(4,128)S(1)} %get-tuple-element.171, f32[512,1024]{1,0:T(8,128)S(1)} %get-tuple-element.147, ...), kind=kLoop, calls=%fused_computation.9.clone.1 | loop fusion | flops 12579840 | bytes 4243456 | tf_op jit(solution)/shard_map/while/body/eval_jaxpr/reduce_sum | solution.py:56
  98.8 1.1 broadcast_subtract_fusion.3
  99.9 2.1 %fusion.19 = (f32[512,1024]{1,0:T(8,128)S(1)}, f32[512,1024]{1,0:T(8,128)S(1)}) fusion(f32[3,512,1024]{2,1,0:T(8,128)S(1)} %get-tuple-element.144, f32[3,512,1024]{2,1,0:T(8,128)S(1)} %get-tuple-element.145, f32[1024]{0:T(1024)S(1)} %bitcast.85), kind=kLoop, calls=%fused_computation.16.clone.1 | loop fusion | flops 8388608 | bytes 16781312 | tf_op jit(solution)/shard_map/while/body/eval_jaxpr/mul | solution.py:57
  102.0 2.4 %multiply_reduce_fusion.3 = (f32[3,512]{1,0:T(4,128)S(1)}, f32[3,512]{1,0:T(4,128)S(1)}) fusion(f32[512,1024]{1,0:T(8,128)S(1)} %get-tuple-element.146, f32[3,512]{1,0:T(4,128)S(1)} %get-tuple-element.143, f32[3,1024]{1,0:T(4,128)S(1)} %get-tuple-element.171, f32[512,1024]{1,0:T(8,128)S(1)} %get-tuple-element.147, ...), kind=kLoop, calls=%fused_computation.9.clone.1 | loop fusion | flops 12579840 | bytes 4243456 | tf_op jit(solution)/shard_map/while/body/eval_jaxpr/reduce_sum | solution.py:56
  104.5 1.1 broadcast_subtract_fusion.3
  105.6 2.1 %fusion.19 = (f32[512,1024]{1,0:T(8,128)S(1)}, f32[512,1024]{1,0:T(8,128)S(1)}) fusion(f32[3,512,1024]{2,1,0:T(8,128)S(1)} %get-tuple-element.144, f32[3,512,1024]{2,1,0:T(8,128)S(1)} %get-tuple-element.145, f32[1024]{0:T(1024)S(1)} %bitcast.85), kind=kLoop, calls=%fused_computation.16.clone.1 | loop fusion | flops 8388608 | bytes 16781312 | tf_op jit(solution)/shard_map/while/body/eval_jaxpr/mul | solution.py:57
  107.7 2.4 %multiply_reduce_fusion.3 = (f32[3,512]{1,0:T(4,128)S(1)}, f32[3,512]{1,0:T(4,128)S(1)}) fusion(f32[512,1024]{1,0:T(8,128)S(1)} %get-tuple-element.146, f32[3,512]{1,0:T(4,128)S(1)} %get-tuple-element.143, f32[3,1024]{1,0:T(4,128)S(1)} %get-tuple-element.171, f32[512,1024]{1,0:T(8,128)S(1)} %get-tuple-element.147, ...), kind=kLoop, calls=%fused_computation.9.clone.1 | loop fusion | flops 12579840 | bytes 4243456 | tf_op jit(solution)/shard_map/while/body/eval_jaxpr/reduce_sum | solution.py:56
  110.2 1.1 broadcast_subtract_fusion.3
  111.2 2.1 %fusion.19 = (f32[512,1024]{1,0:T(8,128)S(1)}, f32[512,1024]{1,0:T(8,128)S(1)}) fusion(f32[3,512,1024]{2,1,0:T(8,128)S(1)} %get-tuple-element.144, f32[3,512,1024]{2,1,0:T(8,128)S(1)} %get-tuple-element.145, f32[1024]{0:T(1024)S(1)} %bitcast.85), kind=kLoop, calls=%fused_computation.16.clone.1 | loop fusion | flops 8388608 | bytes 16781312 | tf_op jit(solution)/shard_map/while/body/eval_jaxpr/mul | solution.py:57
  113.3 2.4 %multiply_reduce_fusion.3 = (f32[3,512]{1,0:T(4,128)S(1)}, f32[3,512]{1,0:T(4,128)S(1)}) fusion(f32[512,1024]{1,0:T(8,128)S(1)} %get-tuple-element.146, f32[3,512]{1,0:T(4,128)S(1)} %get-tuple-element.143, f32[3,1024]{1,0:T(4,128)S(1)} %get-tuple-element.171, f32[512,1024]{1,0:T(8,128)S(1)} %get-tuple-element.147, ...), kind=kLoop, calls=%fused_computation.9.clone.1 | loop fusion | flops 12579840 | bytes 4243456 | tf_op jit(solution)/shard_map/while/body/eval_jaxpr/reduce_sum | solution.py:56
  115.8 1.1 broadcast_subtract_fusion.3
  116.9 2.1 %fusion.19 = (f32[512,1024]{1,0:T(8,128)S(1)}, f32[512,1024]{1,0:T(8,128)S(1)}) fusion(f32[3,512,1024]{2,1,0:T(8,128)S(1)} %get-tuple-element.144, f32[3,512,1024]{2,1,0:T(8,128)S(1)} %get-tuple-element.145, f32[1024]{0:T(1024)S(1)} %bitcast.85), kind=kLoop, calls=%fused_computation.16.clone.1 | loop fusion | flops 8388608 | bytes 16781312 | tf_op jit(solution)/shard_map/while/body/eval_jaxpr/mul | solution.py:57
  119.0 2.4 %multiply_reduce_fusion.3 = (f32[3,512]{1,0:T(4,128)S(1)}, f32[3,512]{1,0:T(4,128)S(1)}) fusion(f32[512,1024]{1,0:T(8,128)S(1)} %get-tuple-element.146, f32[3,512]{1,0:T(4,128)S(1)} %get-tuple-element.143, f32[3,1024]{1,0:T(4,128)S(1)} %get-tuple-element.171, f32[512,1024]{1,0:T(8,128)S(1)} %get-tuple-element.147, ...), kind=kLoop, calls=%fused_computation.9.clone.1 | loop fusion | flops 12579840 | bytes 4243456 | tf_op jit(solution)/shard_map/while/body/eval_jaxpr/reduce_sum | solution.py:56
  124.2 52.9 %reduce-scatter.2.cloned.1.call-done = f32[6,256]{1,0:T(8,128)} async-done(((f32[6,4096]{1,0:T(8,128)}), f32[6,256]{1,0:T(8,128)}) %reduce-scatter.2.cloned.1.call-update) | async-done | bytes 6160 | tf_op jit(solution)/shard_map/reduce_scatter | solution.py:91
  178.8 1.4 scatter_fusion.1
  181.1 1.4 scatter_fusion
  183.3 1.3 maximum_select_fusion
  (93 shorter events, 13.4 us)
Async XLA Ops:
  7.2 170.0 %reduce-scatter.2.cloned.1.call-start = ((), (), s32[]{:S(2)}) async-start(), calls=%async_computation.1 | async-start | bytes 139264 | tf_op jit(solution)/shard_map/reduce_scatter | solution.py:91
  12.6 8.1 %collective-permute-start = (f32[6,256]{0,1:T(8,128)S(1)}, f32[6,256]{0,1:T(8,128)S(1)}, u32[]{:S(2)}, u32[]{:S(2)}) collective-permute-start(f32[6,256]{0,1:T(8,128)S(1)} %bitcast.81), channel_id=1, source_target_pairs={{0,1},{1,2},{2,3},{3,4},{4,5},{5,6},{6,7},{7,8},{8,9},{9,10},{10,1... | collective-permute-start | bytes 18440 | tf_op jit(solution)/shard_map/ppermute | solution.py:25
  20.7 7.1 %collective-permute-start.1 = (f32[6,256]{0,1:T(8,128)S(1)}, f32[6,256]{0,1:T(8,128)S(1)}, u32[]{:S(2)}, u32[]{:S(2)}) collective-permute-start(f32[6,256]{0,1:T(8,128)S(1)} %collective-permute-done), channel_id=1, source_target_pairs={{0,1},{1,2},{2,3},{3,4},{4,5},{5,6},{6,7},{7,8},{8,9},{9,10},{10,1... | collective-permute-start | bytes 18440 | tf_op jit(solution)/shard_map/ppermute | solution.py:25
  20.7 7.1 %collective-permute-start.8 = (f32[6,256]{0,1:T(8,128)S(1)}, f32[6,256]{0,1:T(8,128)S(1)}, u32[]{:S(2)}, u32[]{:S(2)}) collective-permute-start(f32[6,256]{0,1:T(8,128)S(1)} %bitcast.82), channel_id=1, source_target_pairs={{1,0},{2,1},{3,2},{4,3},{5,4},{6,5},{7,6},{8,7},{9,8},{10,9},{11,1... | collective-permute-start | bytes 18440 | tf_op jit(solution)/shard_map/ppermute | solution.py:27
  27.8 7.2 %collective-permute-start.2 = (f32[6,256]{0,1:T(8,128)S(1)}, f32[6,256]{0,1:T(8,128)S(1)}, u32[]{:S(2)}, u32[]{:S(2)}) collective-permute-start(f32[6,256]{0,1:T(8,128)S(1)} %collective-permute-done.1), channel_id=1, source_target_pairs={{0,1},{1,2},{2,3},{3,4},{4,5},{5,6},{6,7},{7,8},{8,9},{9,10},{10,1... | collective-permute-start | bytes 18440 | tf_op jit(solution)/shard_map/ppermute | solution.py:25
  27.8 7.2 %collective-permute-start.9 = (f32[6,256]{0,1:T(8,128)S(1)}, f32[6,256]{0,1:T(8,128)S(1)}, u32[]{:S(2)}, u32[]{:S(2)}) collective-permute-start(f32[6,256]{0,1:T(8,128)S(1)} %collective-permute-done.8), channel_id=1, source_target_pairs={{1,0},{2,1},{3,2},{4,3},{5,4},{6,5},{7,6},{8,7},{9,8},{10,9},{11,1... | collective-permute-start | bytes 18440 | tf_op jit(solution)/shard_map/ppermute | solution.py:27
  35.0 7.2 %collective-permute-start.3 = (f32[6,256]{0,1:T(8,128)S(1)}, f32[6,256]{0,1:T(8,128)S(1)}, u32[]{:S(2)}, u32[]{:S(2)}) collective-permute-start(f32[6,256]{0,1:T(8,128)S(1)} %collective-permute-done.2), channel_id=1, source_target_pairs={{0,1},{1,2},{2,3},{3,4},{4,5},{5,6},{6,7},{7,8},{8,9},{9,10},{10,1... | collective-permute-start | bytes 18440 | tf_op jit(solution)/shard_map/ppermute | solution.py:25
  35.0 7.2 %collective-permute-start.10 = (f32[6,256]{0,1:T(8,128)S(1)}, f32[6,256]{0,1:T(8,128)S(1)}, u32[]{:S(2)}, u32[]{:S(2)}) collective-permute-start(f32[6,256]{0,1:T(8,128)S(1)} %collective-permute-done.9), channel_id=1, source_target_pairs={{1,0},{2,1},{3,2},{4,3},{5,4},{6,5},{7,6},{8,7},{9,8},{10,9},{11,1... | collective-permute-start | bytes 18440 | tf_op jit(solution)/shard_map/ppermute | solution.py:27
  42.2 7.2 %collective-permute-start.4 = (f32[6,256]{0,1:T(8,128)S(1)}, f32[6,256]{0,1:T(8,128)S(1)}, u32[]{:S(2)}, u32[]{:S(2)}) collective-permute-start(f32[6,256]{0,1:T(8,128)S(1)} %collective-permute-done.3), channel_id=1, source_target_pairs={{0,1},{1,2},{2,3},{3,4},{4,5},{5,6},{6,7},{7,8},{8,9},{9,10},{10,1... | collective-permute-start | bytes 18440 | tf_op jit(solution)/shard_map/ppermute | solution.py:25
  42.2 7.2 %collective-permute-start.11 = (f32[6,256]{0,1:T(8,128)S(1)}, f32[6,256]{0,1:T(8,128)S(1)}, u32[]{:S(2)}, u32[]{:S(2)}) collective-permute-start(f32[6,256]{0,1:T(8,128)S(1)} %collective-permute-done.10), channel_id=1, source_target_pairs={{1,0},{2,1},{3,2},{4,3},{5,4},{6,5},{7,6},{8,7},{9,8},{10,9},{11,1... | collective-permute-start | bytes 18440 | tf_op jit(solution)/shard_map/ppermute | solution.py:27
  49.4 7.2 %collective-permute-start.5 = (f32[6,256]{0,1:T(8,128)S(1)}, f32[6,256]{0,1:T(8,128)S(1)}, u32[]{:S(2)}, u32[]{:S(2)}) collective-permute-start(f32[6,256]{0,1:T(8,128)S(1)} %collective-permute-done.4), channel_id=1, source_target_pairs={{0,1},{1,2},{2,3},{3,4},{4,5},{5,6},{6,7},{7,8},{8,9},{9,10},{10,1... | collective-permute-start | bytes 18440 | tf_op jit(solution)/shard_map/ppermute | solution.py:25
  49.4 7.2 %collective-permute-start.12 = (f32[6,256]{0,1:T(8,128)S(1)}, f32[6,256]{0,1:T(8,128)S(1)}, u32[]{:S(2)}, u32[]{:S(2)}) collective-permute-start(f32[6,256]{0,1:T(8,128)S(1)} %collective-permute-done.11), channel_id=1, source_target_pairs={{1,0},{2,1},{3,2},{4,3},{5,4},{6,5},{7,6},{8,7},{9,8},{10,9},{11,1... | collective-permute-start | bytes 18440 | tf_op jit(solution)/shard_map/ppermute | solution.py:27
  56.6 13.1 %copy-start.6 = (f32[6,256]{0,1:T(8,128)}, f32[6,256]{0,1:T(8,128)S(1)}, u32[]{:S(2)}) copy-start(f32[6,256]{0,1:T(8,128)S(1)} %collective-permute-done.5) | copy-start | bytes 18436
  56.6 7.2 %collective-permute-start.6 = (f32[6,256]{0,1:T(8,128)S(1)}, f32[6,256]{0,1:T(8,128)S(1)}, u32[]{:S(2)}, u32[]{:S(2)}) collective-permute-start(f32[6,256]{0,1:T(8,128)S(1)} %collective-permute-done.5), channel_id=1, source_target_pairs={{0,1},{1,2},{2,3},{3,4},{4,5},{5,6},{6,7},{7,8},{8,9},{9,10},{10,1... | collective-permute-start | bytes 18440 | tf_op jit(solution)/shard_map/ppermute | solution.py:25
  56.6 13.0 %copy-start.2 = (f32[6,256]{0,1:T(8,128)}, f32[6,256]{0,1:T(8,128)S(1)}, u32[]{:S(2)}) copy-start(f32[6,256]{0,1:T(8,128)S(1)} %collective-permute-done.12) | copy-start | bytes 18436
  56.6 8.5 %collective-permute-start.13 = (f32[6,256]{0,1:T(8,128)S(1)}, f32[6,256]{0,1:T(8,128)}, u32[]{:S(2)}, u32[]{:S(2)}) collective-permute-start(f32[6,256]{0,1:T(8,128)S(1)} %collective-permute-done.12), channel_id=1, source_target_pairs={{1,0},{2,1},{3,2},{4,3},{5,4},{6,5},{7,6},{8,7},{9,8},{10,9},{11,1... | collective-permute-start | bytes 18440 | tf_op jit(solution)/shard_map/ppermute | solution.py:27
  63.8 5.9 %copy-start.7 = (f32[6,256]{0,1:T(8,128)}, f32[6,256]{0,1:T(8,128)S(1)}, u32[]{:S(2)}) copy-start(f32[6,256]{0,1:T(8,128)S(1)} %collective-permute-done.6) | copy-start | bytes 18436
  63.8 7.2 %collective-permute-start.7 = (f32[6,256]{0,1:T(8,128)S(1)}, f32[6,256]{0,1:T(8,128)}, u32[]{:S(2)}, u32[]{:S(2)}) collective-permute-start(f32[6,256]{0,1:T(8,128)S(1)} %collective-permute-done.6), channel_id=1, source_target_pairs={{0,1},{1,2},{2,3},{3,4},{4,5},{5,6},{6,7},{7,8},{8,9},{9,10},{10,1... | collective-permute-start | bytes 18440 | tf_op jit(solution)/shard_map/ppermute | solution.py:25
  65.2 9.7 %collective-permute-start.14 = (f32[6,256]{0,1:T(8,128)}, f32[6,256]{0,1:T(8,128)S(1)}, u32[]{:S(2)}, u32[]{:S(2)}) collective-permute-start(f32[6,256]{0,1:T(8,128)} %collective-permute-done.13), channel_id=1, source_target_pairs={{1,0},{2,1},{3,2},{4,3},{5,4},{6,5},{7,6},{8,7},{9,8},{10,9},{11,1... | collective-permute-start | bytes 18440 | tf_op jit(solution)/shard_map/ppermute | solution.py:27
  71.0 3.0 %copy-start.3 = (f32[6,256]{0,1:T(8,128)S(1)}, f32[6,256]{0,1:T(8,128)}, u32[]{:S(2)}) copy-start(f32[6,256]{0,1:T(8,128)} %copy-done.2) | copy-start | bytes 18436
  73.9 2.3 %copy-start.4 = (f32[8,6,512]{2,1,0:T(8,128)S(1)}, f32[8,6,512]{2,1,0:T(8,128)}, u32[]{:S(2)}) copy-start(f32[8,6,512]{2,1,0:T(8,128)} %custom-call.11) | copy-start | bytes 294916
  73.9 2.3 %copy-start.8 = (f32[1024]{0:T(1024)S(1)}, f32[1024]{0:T(1024)}, u32[]{:S(2)}) copy-start(f32[1024]{0:T(1024)} %param.11) | copy-start | bytes 12292
  76.2 46.0 %copy-start = (f32[6,1024]{1,0:T(8,128)S(1)}, f32[6,1024]{1,0:T(8,128)}, u32[]{:S(2)}) copy-start(f32[6,1024]{1,0:T(8,128)} %param.10) | copy-start | bytes 73732
  76.2 46.2 %copy-start.1 = (f32[6,1024]{1,0:T(8,128)S(1)}, f32[6,1024]{1,0:T(8,128)}, u32[]{:S(2)}) copy-start(f32[6,1024]{1,0:T(8,128)} %param.9) | copy-start | bytes 73732
  121.4 0.7 copy-start.5
Sparse Core Ops, SparseCore 0:
  122.2 54.8 reduce-scatter.1
